TPU v7x, 32 devices: a whole 2x2x4 slice. The times are simulated.
32 devices in a mesh: seq: 8 (over z, x), ch: 4 (over y, core).
Axes of the slice: x: 2, y: 2, z: 4, core: 2. Of those that a mesh axis runs over, the one named last changes fastest.
Arguments:
- block_input: bfloat16 [131072, 2048], P('seq', 'ch'), may hold values from -6 to 6
- gate_pre: bfloat16 [131072, 2048], P('seq', 'ch'), may hold values from -8 to 8
- out_grad: bfloat16 [131072, 2048], P('seq', 'ch'), may hold values from -6 to 6
- block_weight: bfloat16 [256, 512, 512], P('seq', 'ch'), may hold values from -0.25 to 0.25
- offset_weight: bfloat16 [512, 256, 256], P(('seq', 'ch')), may hold values from -0.375 to 0.375
- out_weight: bfloat16 [2048, 2048], P(None, 'ch'), may hold values from -0.125 to 0.125
- reset_offset: int32 [256], replicated, may hold values from 0 to 512, as said below
Outputs:
- input_grad: bfloat16 [131072, 2048], P('seq', 'ch')
- gate_grad: bfloat16 [131072, 2048], P('seq', 'ch')
- block_grad: bfloat16 [256, 512, 512], P('seq', 'ch')
- offset_grad: bfloat16 [512, 256, 256], P(('seq', 'ch'))
- out_weight_grad: bfloat16 [2048, 2048], P('seq', 'ch')
Inputs may be any that keep to these rules, and one draw needn't show every extreme that they name: reset_offset[0] is 0 and the last block starts no document; other blocks start a document at some place or none.
All inputs are finite; a program needn't handle non-finite values.
Results may differ from a plain program's by a relative error of at most 0.013.
Values may be sent and summed in bfloat16 or wider, within the bound.
No kernel may reach another device: no remote copies, remote signals or barrier semaphores. Data moves between devices by JAX's collectives and lax.ppermute only.
A program may use at most 512 MiB of HBM per device.

v0:
```python
import jax
import jax.numpy as jnp
from jax import lax
from jax.sharding import PartitionSpec as P


def side_flags_of(reset_offset, block_span):
    within = jnp.arange(block_span, dtype=jnp.int32)
    return within[None, :] >= reset_offset[:, None]


def document_ids(reset_offset, block_span):
    starts = (reset_offset < block_span).astype(jnp.int32)
    earlier = jnp.cumsum(starts) - starts
    return earlier[:, None] + side_flags_of(reset_offset, block_span).astype(jnp.int32)


def to_offsets(blocked, seq_count, ch_count):
    block_count, block_span, channels = blocked.shape
    arrived = lax.all_to_all(
        blocked.reshape(1, block_count, block_span, channels),
        ("seq", "ch"),
        split_axis=2,
        concat_axis=0,
        tiled=True,
    )
    return arrived.reshape(
        seq_count, ch_count, block_count, block_span // (seq_count * ch_count), channels
    )


def to_blocks(spread, seq_count, ch_count):
    block_count = spread.shape[2]
    offsets = spread.shape[3]
    channels = spread.shape[4]
    arrived = lax.all_to_all(
        spread.reshape(seq_count * ch_count, block_count, offsets, channels),
        ("seq", "ch"),
        split_axis=0,
        concat_axis=2,
        tiled=True,
    )
    return arrived.reshape(block_count, offsets * seq_count * ch_count, channels)


def on_device(
    block_input, gate_pre, out_grad, block_weight, offset_weight, out_weight, reset_offset
):
    seq_count = lax.axis_size("seq")
    ch_count = lax.axis_size("ch")
    token_count, channels = block_input.shape
    block_span = block_weight.shape[2]
    block_count = token_count // block_span
    offsets = block_span // (seq_count * ch_count)
    full_grad, full_weight = (
        lax.all_gather(out_grad, "ch", axis=1, tiled=True),
        lax.all_gather(block_weight, "ch", axis=1, tiled=True),
    )
    seq_index = lax.axis_index("seq")
    flat_index = seq_index * ch_count + lax.axis_index("ch")
    side_table = side_flags_of(reset_offset, block_span)
    doc_table = document_ids(reset_offset, block_span)
    total_blocks = doc_table.shape[0]
    local_sides = lax.dynamic_slice_in_dim(side_table, seq_index * block_count, block_count, 0)
    mask_one = local_sides[:, :, None] == local_sides[:, None, :]
    masked_one = jnp.where(mask_one, full_weight, jnp.zeros_like(full_weight))
    inputs = block_input.reshape(block_count, block_span, channels)
    section_out = jnp.einsum(
        "ikj,ijd->ikd", masked_one, inputs, preferred_element_type=jnp.float32
    ).astype(jnp.bfloat16)
    section_spread = to_offsets(section_out, seq_count, ch_count)
    labels = lax.dynamic_slice_in_dim(doc_table, flat_index * offsets, offsets, 1).T
    mask_two = labels[:, :, None] == labels[:, None, :]
    masked_two = jnp.where(mask_two, offset_weight, jnp.zeros_like(offset_weight))
    masked_two = masked_two.reshape(offsets, seq_count, block_count, seq_count, block_count)
    mixer_spread = jnp.einsum(
        "kpqsi,scikd->pcqkd", masked_two, section_spread, preferred_element_type=jnp.float32
    ).astype(jnp.bfloat16)
    mixer_out = to_blocks(mixer_spread, seq_count, ch_count).reshape(token_count, channels)
    head_grad = jnp.dot(full_grad, out_weight, preferred_element_type=jnp.float32)
    sigmoid_gate = jax.nn.sigmoid(gate_pre.astype(jnp.float32))
    mixer_float = mixer_out.astype(jnp.float32)
    gated_out = (mixer_float * sigmoid_gate).astype(jnp.bfloat16)
    weight_share = lax.psum_scatter(
        jnp.einsum("te,tc->ec", full_grad, gated_out, preferred_element_type=jnp.float32).astype(
            jnp.bfloat16
        ),
        "seq",
        scatter_dimension=0,
        tiled=True,
    )
    mixer_grad = (head_grad * sigmoid_gate).astype(jnp.bfloat16)
    gate_grad = (head_grad * mixer_float * sigmoid_gate * (1.0 - sigmoid_gate)).astype(jnp.bfloat16)
    grad_spread = to_offsets(
        mixer_grad.reshape(block_count, block_span, channels), seq_count, ch_count
    )
    offset_grad = jnp.einsum(
        "pcqkd,scikd->kpqsi", grad_spread, section_spread, preferred_element_type=jnp.float32
    ).reshape(offsets, total_blocks, total_blocks)
    section_grad_spread = jnp.einsum(
        "kpqsi,pcqkd->scikd", masked_two, grad_spread, preferred_element_type=jnp.float32
    ).astype(jnp.bfloat16)
    offset_grad = jnp.where(mask_two, offset_grad, jnp.zeros_like(offset_grad)).astype(jnp.bfloat16)
    section_grad = to_blocks(section_grad_spread, seq_count, ch_count)
    partial_grad = jnp.einsum(
        "ikd,ijd->ikj", section_grad, inputs, preferred_element_type=jnp.float32
    )
    partial_grad = jnp.where(mask_one, partial_grad, jnp.zeros_like(partial_grad))
    block_grad = lax.psum_scatter(
        partial_grad.astype(jnp.bfloat16), "ch", scatter_dimension=1, tiled=True
    )
    input_grad = jnp.einsum(
        "ikj,ikd->ijd", masked_one, section_grad, preferred_element_type=jnp.float32
    ).astype(jnp.bfloat16)
    return (
        input_grad.reshape(token_count, channels),
        gate_grad,
        block_grad,
        offset_grad,
        weight_share,
    )


def solution(mesh):
    in_specs = (
        P("seq", "ch"),
        P("seq", "ch"),
        P("seq", "ch"),
        P("seq", "ch", None),
        P(("seq", "ch"), None, None),
        P(None, "ch"),
        P(),
    )
    out_specs = (
        P("seq", "ch"),
        P("seq", "ch"),
        P("seq", "ch", None),
        P(("seq", "ch"), None, None),
        P("seq", "ch"),
    )
    return jax.shard_map(
        on_device, mesh=mesh, in_specs=in_specs, out_specs=out_specs, check_vma=False
    )
```

profile of v0, /device:TPU:6, one launch (start us, length us, event | category | flops | bytes accessed | tf_op | source)
XLA Modules:
  0.0 2105.8 jit_solution(565953672333166698)
XLA Ops:
  7.2 0.0 copy-start
  7.2 0.0 all-gather.3.cloned.1.call-start
  7.2 0.7 all-gather.3.cloned.1.call-update
  7.9 0.0 all-gather.5.cloned.1.call-start
  8.0 0.7 all-gather.5.cloned.1.call-update
  8.7 0.1 iota_compare_fusion
  8.9 0.0 copy-start.4
  8.9 106.9 %all-gather.3.cloned.1.call-done = bf16[32,512,512]{2,1,0:T(8,128)(2,1)} async-done(((bf16[32,128,512]{2,1,0:T(8,128)(2,1)}), bf16[32,512,512]{2,1,0:T(8,128)(2,1)}) %all-gather.3.cloned.1.call-update) | async-done | bytes 16777232 | tf_op jit(solution)/shard_map/all_gather | solution.py:57
  115.8 26.4 %convert_bitcast_fusion.1 = bf16[1,32,512,512]{3,2,1,0:T(8,128)(2,1)} fusion(bf16[32,512,512]{2,1,0:T(8,128)(2,1)} %bitcast.95, bf16[32,512,512]{2,1,0:T(8,128)(2,1)} %all-gather.3.cloned.1.call-done, pred[32,512]{1,0:T(8,128)(4,1)S(1)} %constant_dynamic-slice_fusion), kind=kOutput, calls=%fused_computation.23 | convolution fusion | flops 8615100416 | bytes 50348032 | tf_op jit(solution)/shard_map/ikj,ijd->ikd/dot_general | solution.py:68
  142.1 20.2 copy.82
  162.3 6.2 all-to-all-start.2
  168.6 0.3 reduce-window.9
  168.9 0.1 slice.7
  169.0 0.1 slice_reduce_fusion
  169.2 0.1 bitcast_subtract_fusion
  169.2 0.1 add_bitcast_fusion
  169.4 0.1 copy.75
  169.4 2.9 compare_select_fusion.9
  172.4 10.0 reshape.71
  182.4 364.9 %all-to-all-done.2 = bf16[1,32,512,512]{3,1,0,2:T(8,128)(2,1)} async-done(((bf16[1,32,512,512]{3,1,0,2:T(8,128)(2,1)}), bf16[1,32,512,512]{3,1,0,2:T(8,128)(2,1)}, u32[]{:S(2)}, u32[]{:S(2)}) %all-to-all-start.2) | async-done | bytes 16777248 | tf_op jit(solution)/shard_map/all_to_all | solution.py:20
  547.3 16.9 copy.83
  564.2 37.1 %fusion.6 = bf16[8,4,32,16,512]{4,2,0,1,3:T(8,128)(2,1)} fusion(bf16[8,4,32,16,512,1]{4,3,1,0,2,5:T(8,128)(2,1)} %bitcast.90, bf16[16,8,32,8,32,1]{4,3,2,1,0,5:T(8,128)(2,1)} %bitcast.88), kind=kOutput, calls=%fused_computation.15 | convolution fusion | flops 4303355904 | bytes 35651584 | tf_op jit(solution)/shard_map/kpqsi,scikd->pcqkd/dot_general | solution.py:76
  601.3 15.9 copy.87
  617.2 365.9 %all_to_all.54 = bf16[32,32,16,512]{3,2,1,0:T(8,128)(2,1)} all-to-all(bf16[32,32,16,512]{3,2,1,0:T(8,128)(2,1)S(1)} %bitcast.87), channel_id=1, replica_groups=mesh['seq'=8,'ch'=4] {'seq','ch'}, dimensions={0} | all-to-all | bytes 33554432 | tf_op jit(solution)/shard_map/all_to_all | solution.py:36
  983.2 9.9 convert_bitcast_fusion
  993.0 11.6 copy.88
  1004.6 63.6 %fusion.4 = (bf16[16384,512]{1,0:T(8,128)(2,1)}, bf16[16384,512]{1,0:T(8,128)(2,1)}, bf16[16384,512]{1,0:T(8,128)(2,1)}) fusion(f32[1,32,32,16,512]{4,3,2,1,0:T(8,128)} %copy.88, bf16[16384,512]{1,0:T(8,128)(2,1)} %param.8, bf16[16384,2048]{1,0:T(8,128)(2,1)} %all-gather.5.cloned.1.call-done, bf16[2048,512]{1,0:T(8,128)(2,1)S(1)} %copy-done), kind=kOutput, calls=%fused_computation.9 | convolution fusion | flops 34468790272 | bytes 169869312 | tf_op jit(solution)/shard_map/dot_general | solution.py:80
  1068.2 15.9 copy.72
  1084.1 367.1 %all_to_all.55 = bf16[1,32,512,512]{3,1,0,2:T(8,128)(2,1)S(1)} all-to-all(bf16[1,32,512,512]{3,1,0,2:T(8,128)(2,1)S(1)} %copy.72), channel_id=1, replica_groups=mesh['seq'=8,'ch'=4] {'seq','ch'}, dimensions={2} | all-to-all | bytes 33554432 | tf_op jit(solution)/shard_map/all_to_all | solution.py:20
  1451.2 20.5 copy.73
  1471.8 35.7 %fusion.5 = bf16[8,4,32,16,512]{4,2,0,1,3:T(8,128)(2,1)} fusion(bf16[8,4,32,16,512,1]{4,3,1,0,2,5:T(8,128)(2,1)} %bitcast.84, bf16[16,8,32,8,32,1]{4,3,2,1,0,5:T(8,128)(2,1)} %bitcast.89), kind=kOutput, calls=%fused_computation.14 | convolution fusion | flops 4303355904 | bytes 35651584 | tf_op jit(solution)/shard_map/kpqsi,pcqkd->scikd/dot_general | solution.py:100
  1507.4 18.5 copy.79
  1525.9 4.2 all-to-all-start.1
  1530.1 0.0 reduce-scatter.5.cloned.1.call-start
  1530.1 44.5 %fusion.31 = bf16[2048,512]{0,1:T(8,128)(2,1)} fusion(bf16[16384,512]{1,0:T(8,128)(2,1)} %get-tuple-element.30, bf16[16384,2048]{1,0:T(8,128)(2,1)} %all-gather.5.cloned.1.call-done), kind=kOutput, calls=%fused_computation.36 | convolution fusion | flops 34360786944 | bytes 85983232 | tf_op jit(solution)/shard_map/te,tc->ec/dot_general | solution.py:85
  1574.6 0.0 reduce-scatter.5.cloned.1.call-update
  1574.6 0.0 reduce-scatter.3.cloned.1.call-start
  1574.6 350.6 %all-to-all-done.1 = bf16[32,32,16,512]{3,2,1,0:T(8,128)(2,1)} async-done(((bf16[32,32,16,512]{3,2,1,0:T(8,128)(2,1)}), bf16[32,32,16,512]{3,2,1,0:T(8,128)(2,1)}, u32[]{:S(2)}, u32[]{:S(2)}) %all-to-all-start.1) | async-done | bytes 16777248 | tf_op jit(solution)/shard_map/all_to_all | solution.py:36
  1925.3 14.1 copy.80
  1939.4 21.5 %fusion = bf16[32,512,512]{2,1,0:T(8,128)(2,1)} fusion(pred[32,512]{1,0:T(8,128)(4,1)S(1)} %copy-done.5, bf16[32,512,512]{2,1,0:T(8,128)(2,1)} %bitcast.92, bf16[32,512,512]{2,1,0:T(8,128)(2,1)} %bitcast.96), kind=kOutput, calls=%fused_computation.2 | convolution fusion | flops 8615100416 | bytes 50348032 | tf_op jit(solution)/shard_map/ikd,ijd->ikj/dot_general | solution.py:105
  1960.9 0.0 reduce-scatter.3.cloned.1.call-update
  1960.9 0.0 reduce-scatter.5.cloned.1.call-done
  1961.0 1.8 copy.92
  1962.8 85.1 %fusion.21 = bf16[16,8,32,8,32]{4,2,3,1,0:T(8,128)(2,1)} fusion(bf16[8,4,32,16,512,1]{4,3,1,0,2,5:T(8,128)(2,1)} %bitcast.91, bf16[8,4,32,16,512,1]{4,3,1,0,2,5:T(8,128)(2,1)} %bitcast.85), kind=kOutput, calls=%fused_computation.27 | convolution fusion | flops 4294967296 | bytes 35651584 | tf_op jit(solution)/shard_map/pcqkd,scikd->kpqsi/dot_general | solution.py:97
  2047.9 15.5 copy.91
  2063.4 9.8 reshape.79
  2073.2 1.7 fusion.30
  2074.9 23.9 %fusion.16 = bf16[32,512,512]{2,1,0:T(8,128)(2,1)} fusion(bf16[32,512,512]{2,1,0:T(8,128)(2,1)} %bitcast.93, bf16[32,512,512]{2,1,0:T(8,128)(2,1)} %all-gather.3.cloned.1.call-done, pred[32,512]{1,0:T(8,128)(4,1)S(1)} %copy-done.5), kind=kOutput, calls=%fused_computation.26 | convolution fusion | flops 8615100416 | bytes 50348032 | tf_op jit(solution)/shard_map/ikj,ikd->ijd/dot_general | solution.py:112
  (17 shorter events, 0.1 us)
Async XLA Ops:
  7.2 997.5 %copy-start = (bf16[2048,512]{1,0:T(8,128)(2,1)S(1)}, bf16[2048,512]{1,0:T(8,128)(2,1)}, u32[]{:S(2)}) copy-start(bf16[2048,512]{1,0:T(8,128)(2,1)} %param.12) | copy-start | bytes 6291460
  7.2 1.5 copy-start.6
  7.2 108.6 %all-gather.3.cloned.1.call-start = ((), (), s32[]{:S(2)}) async-start(), calls=%async_computation.6 | async-start | bytes 20971520 | tf_op jit(solution)/shard_map/all_gather | solution.py:57
  7.9 996.7 %all-gather.5.cloned.1.call-start = ((), (), s32[]{:S(2)}) async-start(), calls=%async_computation.7 | async-start | bytes 83886080 | tf_op jit(solution)/shard_map/all_gather | solution.py:56
  8.9 133.3 %copy-start.4 = (pred[32,512]{1,0:T(8,128)(4,1)}, pred[32,512]{1,0:T(8,128)(4,1)S(1)}, u32[]{:S(2)}) copy-start(pred[32,512]{1,0:T(8,128)(4,1)S(1)} %constant_dynamic-slice_fusion) | copy-start | bytes 49156
  162.3 385.0 %all-to-all-start.2 = ((bf16[1,32,512,512]{3,1,0,2:T(8,128)(2,1)}), bf16[1,32,512,512]{3,1,0,2:T(8,128)(2,1)}, u32[]{:S(2)}, u32[]{:S(2)}) async-start(bf16[1,32,512,512]{3,1,0,2:T(8,128)(2,1)} %copy.82), calls=%async_computation.2 | async-start | bytes 33554432 | tf_op jit(solution)/shard_map/all_to_all | solution.py:20
  169.4 394.8 %copy-start.2 = (s32[16,256]{1,0:T(8,128)}, s32[16,256]{1,0:T(8,128)S(1)}, u32[]{:S(2)}) copy-start(s32[16,256]{1,0:T(8,128)S(1)} %copy.75) | copy-start | bytes 49156
  1525.9 399.4 %all-to-all-start.1 = ((bf16[32,32,16,512]{3,2,1,0:T(8,128)(2,1)}), bf16[32,32,16,512]{3,2,1,0:T(8,128)(2,1)}, u32[]{:S(2)}, u32[]{:S(2)}) async-start(bf16[32,32,16,512]{3,2,1,0:T(8,128)(2,1)} %bitcast.86), calls=%async_computation.1 | async-start | bytes 33554432 | tf_op jit(solution)/shard_map/all_to_all | solution.py:36
  1530.1 430.9 %reduce-scatter.5.cloned.1.call-start = ((), (), s32[]{:S(2)}) async-start(), calls=%async_computation.9 | async-start | bytes 2359296 | tf_op jit(solution)/shard_map/reduce_scatter | solution.py:84
  1574.6 524.2 %reduce-scatter.3.cloned.1.call-start = ((), (), s32[]{:S(2)}) async-start(), calls=%async_computation.8 | async-start | bytes 20971520 | tf_op jit(solution)/shard_map/reduce_scatter | solution.py:109
  1925.3 14.1 copy-start.5
  2047.9 25.3 %copy-start.3 = (s32[16,256]{1,0:T(8,128)S(1)}, s32[16,256]{1,0:T(8,128)}, u32[]{:S(2)}) copy-start(s32[16,256]{1,0:T(8,128)} %copy-done.2) | copy-start | bytes 49156
  2074.9 23.9 %copy-start.1 = (bf16[2048,512]{1,0:T(8,128)(2,1)S(1)}, bf16[2048,512]{1,0:T(8,128)(2,1)}, u32[]{:S(2)}) copy-start(bf16[2048,512]{1,0:T(8,128)(2,1)} %param.12) | copy-start | bytes 6291460
Sparse Core Ops, SparseCore 0:
  9.6 106.1 all-gather.2
  117.3 712.8 all-gather.4
  1574.7 177.2 reduce-scatter.4
  1961.1 122.2 reduce-scatter.2
where the time goes:
time: 2110 us
  waiting for transfers between devices  824 us (39%)
  blocking collectives  733 us (35%)
  matrix products  338 us (16%)
  local copies, waits for them, and re-layouts  171 us (8%)
    all_to_all x1, blocking collectives, to_offsets(): lax.all_to_all(blocked.reshape(1, block_count, block_span, channels), ('s...  367 us
    all_to_all x1, blocking collectives, to_blocks(): lax.all_to_all(spread.reshape(seq_count * ch_count, block_count, offsets,...  366 us
    all_to_all x1, waiting for transfers between devices, to_offsets(): lax.all_to_all(blocked.reshape(1, block_count, block_span, channels), ('s...  365 us
    all_to_all x1, waiting for transfers between devices, to_blocks(): lax.all_to_all(spread.reshape(seq_count * ch_count, block_count, offsets,...  351 us
    all_gather x1, waiting for transfers between devices, on_device(): lax.all_gather(block_weight, 'ch', axis=1, tiled=True)  107 us
    dot_general x1, matrix products, on_device(): jnp.einsum('pcqkd,scikd->kpqsi', grad_spread, section_spread, preferred_e...  85.1 us
    dot_general x1, matrix products, on_device(): jnp.dot(full_grad, out_weight, preferred_element_type=jnp.float32)  63.6 us
    dot_general x1, matrix products, on_device(): jnp.einsum('te,tc->ec', full_grad, gated_out, preferred_element_type=jnp....  44.5 us
  transfers between devices with their start and end apart: 6, of which 3 were waited for; matrix products, arithmetic and copies ran while one was open for 18% of the time, Pallas kernels for 0%

commit v1 on v0

--- a/solution.py
+++ b/solution.py
@@ -33,12 +33,20 @@
     block_count = spread.shape[2]
     offsets = spread.shape[3]
     channels = spread.shape[4]
-    arrived = lax.all_to_all(
-        spread.reshape(seq_count * ch_count, block_count, offsets, channels),
-        ("seq", "ch"),
-        split_axis=0,
-        concat_axis=2,
-        tiled=True,
+    arrived = jnp.concatenate(
+        lax.all_to_all(
+            jnp.stack(
+                jnp.split(
+                    spread.reshape(seq_count * ch_count, block_count, offsets, channels),
+                    lax.axis_size(("seq", "ch")),
+                    axis=0,
+                )
+            ),
+            ("seq", "ch"),
+            0,
+            0,
+        ),
+        axis=2,
     )
     return arrived.reshape(block_count, offsets * seq_count * ch_count, channels)
 

time: 2110 us -> 2140 us (1.014)
  local copies, waits for them, and re-layouts: 171 us -> 196 us
    unnamed x15 -> x77, local copies, waits for them, and re-layouts: 1.83 us -> 28.9 us
  transfers between devices with their start and end apart: 6 -> 6, of which waited for: 3 -> 3; matrix products, arithmetic and copies ran while one was open for 18% -> 17% of each run, Pallas kernels for 0% -> 0%
where the time goes in v1:
time: 2140 us; the launch traced here: 2130 us
  waiting for transfers between devices  825 us (39%)
  blocking collectives  733 us (34%)
  matrix products  337 us (16%)
  local copies, waits for them, and re-layouts  196 us (9%)
    all_to_all x1, blocking collectives, to_offsets(): lax.all_to_all(blocked.reshape(1, block_count, block_span, channels), ('s...  367 us
    all_to_all x1, blocking collectives, to_blocks(): lax.all_to_all(jnp.stack(jnp.split(spread.reshape(seq_count * ch_count, b...  366 us
    all_to_all x1, waiting for transfers between devices, to_offsets(): lax.all_to_all(blocked.reshape(1, block_count, block_span, channels), ('s...  365 us
    all_to_all x1, waiting for transfers between devices, to_blocks(): lax.all_to_all(jnp.stack(jnp.split(spread.reshape(seq_count * ch_count, b...  352 us
    all_gather x1, waiting for transfers between devices, on_device(): lax.all_gather(block_weight, 'ch', axis=1, tiled=True)  107 us
    dot_general x1, matrix products, on_device(): jnp.einsum('pcqkd,scikd->kpqsi', grad_spread, section_spread, preferred_e...  85.1 us
    dot_general x1, matrix products, on_device(): jnp.dot(full_grad, out_weight, preferred_element_type=jnp.float32)  63.6 us
    dot_general x1, matrix products, on_device(): jnp.einsum('te,tc->ec', full_grad, gated_out, preferred_element_type=jnp....  44.1 us
  transfers between devices with their start and end apart: 6, of which 3 were waited for; matrix products, arithmetic and copies ran while one was open for 17% of the time, Pallas kernels for 0%

profile of v1, /device:TPU:6, one launch (start us, length us, event | category | flops | bytes accessed | tf_op | source)
XLA Modules:
  0.0 2132.2 jit_solution(4094296755905292350)
XLA Ops:
  8.9 106.9 %all-gather.3.cloned.1.call-done = bf16[32,512,512]{2,1,0:T(8,128)(2,1)} async-done(((bf16[32,128,512]{2,1,0:T(8,128)(2,1)}), bf16[32,512,512]{2,1,0:T(8,128)(2,1)}) %all-gather.3.cloned.1.call-update) | async-done | bytes 16777232 | tf_op jit(solution)/shard_map/all_gather | solution.py:65
  115.8 26.4 %convert_bitcast_fusion.1 = bf16[1,32,512,512]{3,2,1,0:T(8,128)(2,1)} fusion(bf16[32,512,512]{2,1,0:T(8,128)(2,1)} %bitcast.408, bf16[32,512,512]{2,1,0:T(8,128)(2,1)} %all-gather.3.cloned.1.call-done, pred[32,512]{1,0:T(8,128)(4,1)S(1)} %constant_dynamic-slice_fusion), kind=kOutput, calls=%fused_computation.23 | convolution fusion | flops 8615100416 | bytes 50348032 | tf_op jit(solution)/shard_map/ikj,ijd->ikd/dot_general | solution.py:76
  142.1 20.2 copy.144
  162.3 6.2 all-to-all-start.2
  169.4 2.9 compare_select_fusion.9
  172.4 10.0 reshape.68
  182.4 364.9 %all-to-all-done.2 = bf16[1,32,512,512]{3,1,0,2:T(8,128)(2,1)} async-done(((bf16[1,32,512,512]{3,1,0,2:T(8,128)(2,1)}), bf16[1,32,512,512]{3,1,0,2:T(8,128)(2,1)}, u32[]{:S(2)}, u32[]{:S(2)}) %all-to-all-start.2) | async-done | bytes 16777248 | tf_op jit(solution)/shard_map/all_to_all | solution.py:20
  547.3 16.9 copy.145
  564.2 37.1 %fusion.6 = bf16[8,4,32,16,512]{4,2,0,1,3:T(8,128)(2,1)} fusion(bf16[8,4,32,16,512,1]{4,3,1,0,2,5:T(8,128)(2,1)} %bitcast.403, bf16[16,8,32,8,32,1]{4,3,2,1,0,5:T(8,128)(2,1)} %bitcast.401), kind=kOutput, calls=%fused_computation.15 | convolution fusion | flops 4303355904 | bytes 35651584 | tf_op jit(solution)/shard_map/kpqsi,scikd->pcqkd/dot_general | solution.py:84
  601.3 15.9 copy.149
  618.6 365.9 %all_to_all.40 = bf16[32,1,32,16,512]{4,3,2,1,0:T(8,128)(2,1)} all-to-all(bf16[32,1,32,16,512]{4,3,2,1,0:T(8,128)(2,1)S(1)} %fusion.32), channel_id=1, replica_groups=mesh['seq'=8,'ch'=4] {'seq','ch'}, dimensions={0} | all-to-all | bytes 33554432 | tf_op jit(solution)/shard_map/all_to_all | solution.py:37
  984.6 9.9 convert_bitcast_fusion
  994.4 11.6 copy.150
  1006.1 63.6 %fusion.4 = (bf16[16384,512]{1,0:T(8,128)(2,1)}, bf16[16384,512]{1,0:T(8,128)(2,1)}, bf16[16384,512]{1,0:T(8,128)(2,1)}) fusion(f32[1,32,32,16,512]{4,3,2,1,0:T(8,128)} %copy.150, bf16[16384,512]{1,0:T(8,128)(2,1)} %param.8, bf16[16384,2048]{1,0:T(8,128)(2,1)} %all-gather.5.cloned.1.call-done, bf16[2048,512]{1,0:T(8,128)(2,1)S(1)} %copy-done), kind=kOutput, calls=%fused_computation.8 | convolution fusion | flops 34468790272 | bytes 169869312 | tf_op jit(solution)/shard_map/dot_general | solution.py:88
  1069.6 15.9 copy.134
  1085.5 367.1 %all_to_all.41 = bf16[1,32,512,512]{3,1,0,2:T(8,128)(2,1)S(1)} all-to-all(bf16[1,32,512,512]{3,1,0,2:T(8,128)(2,1)S(1)} %copy.134), channel_id=1, replica_groups=mesh['seq'=8,'ch'=4] {'seq','ch'}, dimensions={2} | all-to-all | bytes 33554432 | tf_op jit(solution)/shard_map/all_to_all | solution.py:20
  1452.6 20.5 copy.135
  1473.2 35.7 %fusion.5 = bf16[8,4,32,16,512]{4,2,0,1,3:T(8,128)(2,1)} fusion(bf16[8,4,32,16,512,1]{4,3,1,0,2,5:T(8,128)(2,1)} %bitcast.399, bf16[16,8,32,8,32,1]{4,3,2,1,0,5:T(8,128)(2,1)} %bitcast.402), kind=kOutput, calls=%fused_computation.14 | convolution fusion | flops 4303355904 | bytes 35651584 | tf_op jit(solution)/shard_map/kpqsi,pcqkd->scikd/dot_general | solution.py:108
  1508.9 15.9 copy.141
  1524.8 0.8 fusion.95
  1525.7 0.8 fusion.94
  1526.5 0.9 fusion.93
  1528.2 0.9 fusion.91
  1529.0 0.8 fusion.90
  1531.5 0.8 fusion.87
  1533.2 0.9 fusion.85
  1535.7 0.8 fusion.82
  1537.3 0.9 fusion.80
  1538.2 0.9 fusion.79
  1539.1 0.8 fusion.78
  1539.9 0.8 fusion.77
  1543.2 0.8 fusion.73
  1544.0 0.8 fusion.72
  1544.9 0.9 fusion.71
  1545.8 0.9 fusion.70
  1548.3 0.8 fusion.67
  1550.8 0.9 fusion.64
  1551.6 4.2 all-to-all-start.1
  1555.8 44.1 %fusion.31 = bf16[2048,512]{0,1:T(8,128)(2,1)} fusion(bf16[16384,512]{1,0:T(8,128)(2,1)} %get-tuple-element.30, bf16[16384,2048]{1,0:T(8,128)(2,1)} %all-gather.5.cloned.1.call-done), kind=kOutput, calls=%fused_computation.36 | convolution fusion | flops 34360786944 | bytes 85983232 | tf_op jit(solution)/shard_map/te,tc->ec/dot_general | solution.py:93
  1600.0 351.7 %all-to-all-done.1 = bf16[32,1,32,16,512]{4,3,2,1,0:T(8,128)(2,1)} async-done(((bf16[32,1,32,16,512]{4,3,2,1,0:T(8,128)(2,1)}), bf16[32,1,32,16,512]{4,3,2,1,0:T(8,128)(2,1)}, u32[]{:S(2)}, u32[]{:S(2)}) %all-to-all-start.1) | async-done | bytes 16777248 | tf_op jit(solution)/shard_map/all_to_all | solution.py:37
  1951.7 14.1 copy.142
  1965.8 21.5 %fusion = bf16[32,512,512]{2,1,0:T(8,128)(2,1)} fusion(pred[32,512]{1,0:T(8,128)(4,1)S(1)} %copy-done.5, bf16[32,512,512]{2,1,0:T(8,128)(2,1)} %bitcast.405, bf16[32,512,512]{2,1,0:T(8,128)(2,1)} %bitcast.409), kind=kOutput, calls=%fused_computation.2 | convolution fusion | flops 8615100416 | bytes 50348032 | tf_op jit(solution)/shard_map/ikd,ijd->ikj/dot_general | solution.py:113
  1987.3 1.8 copy.154
  1989.1 85.1 %fusion.21 = bf16[16,8,32,8,32]{4,2,3,1,0:T(8,128)(2,1)} fusion(bf16[8,4,32,16,512,1]{4,3,1,0,2,5:T(8,128)(2,1)} %bitcast.404, bf16[8,4,32,16,512,1]{4,3,1,0,2,5:T(8,128)(2,1)} %bitcast.400), kind=kOutput, calls=%fused_computation.27 | convolution fusion | flops 4294967296 | bytes 35651584 | tf_op jit(solution)/shard_map/pcqkd,scikd->kpqsi/dot_general | solution.py:105
  2074.3 15.5 copy.153
  2089.8 9.8 reshape.76
  2099.6 1.7 fusion.30
  2101.3 23.9 %fusion.16 = bf16[32,512,512]{2,1,0:T(8,128)(2,1)} fusion(bf16[32,512,512]{2,1,0:T(8,128)(2,1)} %bitcast.406, bf16[32,512,512]{2,1,0:T(8,128)(2,1)} %all-gather.3.cloned.1.call-done, pred[32,512]{1,0:T(8,128)(4,1)S(1)} %copy-done.5), kind=kOutput, calls=%fused_computation.26 | convolution fusion | flops 8615100416 | bytes 50348032 | tf_op jit(solution)/shard_map/ikj,ikd->ijd/dot_general | solution.py:120
  (81 shorter events, 15.3 us)
Async XLA Ops:
  7.2 998.9 %copy-start = (bf16[2048,512]{1,0:T(8,128)(2,1)S(1)}, bf16[2048,512]{1,0:T(8,128)(2,1)}, u32[]{:S(2)}) copy-start(bf16[2048,512]{1,0:T(8,128)(2,1)} %param.12) | copy-start | bytes 6291460
  7.2 1.5 copy-start.6
  7.2 108.6 %all-gather.3.cloned.1.call-start = ((), (), s32[]{:S(2)}) async-start(), calls=%async_computation.6 | async-start | bytes 20971520 | tf_op jit(solution)/shard_map/all_gather | solution.py:65
  7.9 998.1 %all-gather.5.cloned.1.call-start = ((), (), s32[]{:S(2)}) async-start(), calls=%async_computation.7 | async-start | bytes 83886080 | tf_op jit(solution)/shard_map/all_gather | solution.py:64
  8.9 133.3 %copy-start.4 = (pred[32,512]{1,0:T(8,128)(4,1)}, pred[32,512]{1,0:T(8,128)(4,1)S(1)}, u32[]{:S(2)}) copy-start(pred[32,512]{1,0:T(8,128)(4,1)S(1)} %constant_dynamic-slice_fusion) | copy-start | bytes 49156
  162.3 385.0 %all-to-all-start.2 = ((bf16[1,32,512,512]{3,1,0,2:T(8,128)(2,1)}), bf16[1,32,512,512]{3,1,0,2:T(8,128)(2,1)}, u32[]{:S(2)}, u32[]{:S(2)}) async-start(bf16[1,32,512,512]{3,1,0,2:T(8,128)(2,1)} %copy.144), calls=%async_computation.2 | async-start | bytes 33554432 | tf_op jit(solution)/shard_map/all_to_all | solution.py:20
  169.4 394.8 %copy-start.2 = (s32[16,256]{1,0:T(8,128)}, s32[16,256]{1,0:T(8,128)S(1)}, u32[]{:S(2)}) copy-start(s32[16,256]{1,0:T(8,128)S(1)} %copy.137) | copy-start | bytes 49156
  1551.6 400.0 %all-to-all-start.1 = ((bf16[32,1,32,16,512]{4,3,2,1,0:T(8,128)(2,1)}), bf16[32,1,32,16,512]{4,3,2,1,0:T(8,128)(2,1)}, u32[]{:S(2)}, u32[]{:S(2)}) async-start(bf16[32,1,32,16,512]{4,3,2,1,0:T(8,128)(2,1)} %fusion.64), calls=%async_computation.1 | async-start | bytes 33554432 | tf_op jit(solution)/shard_map/all_to_all | solution.py:37
  1555.8 431.6 %reduce-scatter.5.cloned.1.call-start = ((), (), s32[]{:S(2)}) async-start(), calls=%async_computation.9 | async-start | bytes 2359296 | tf_op jit(solution)/shard_map/reduce_scatter | solution.py:92
  1599.9 525.3 %reduce-scatter.3.cloned.1.call-start = ((), (), s32[]{:S(2)}) async-start(), calls=%async_computation.8 | async-start | bytes 20971520 | tf_op jit(solution)/shard_map/reduce_scatter | solution.py:117
  1951.7 14.1 copy-start.5
  2074.3 25.3 %copy-start.3 = (s32[16,256]{1,0:T(8,128)S(1)}, s32[16,256]{1,0:T(8,128)}, u32[]{:S(2)}) copy-start(s32[16,256]{1,0:T(8,128)} %copy-done.2) | copy-start | bytes 49156
  2101.3 23.9 %copy-start.1 = (bf16[2048,512]{1,0:T(8,128)(2,1)S(1)}, bf16[2048,512]{1,0:T(8,128)(2,1)}, u32[]{:S(2)}) copy-start(bf16[2048,512]{1,0:T(8,128)(2,1)} %param.12) | copy-start | bytes 6291460
Sparse Core Ops, SparseCore 0:
  9.6 106.1 all-gather.2
  117.3 712.8 all-gather.4
  1600.0 177.9 reduce-scatter.4
  1987.4 122.2 reduce-scatter.2
